TPU v7x, 32 devices: a whole 2x2x4 slice. The times are simulated.
32 devices in a mesh: pp: 4 (over y, x), cp: 4 (over z), tp: 2 (over core).
Axes of the slice: x: 2, y: 2, z: 4, core: 2. Of those that a mesh axis runs over, the one named last changes fastest.
Arguments:
- queries: bfloat16 [2048, 16384], P(('pp', 'cp'), 'tp'), may hold values from -12 to 12
- keys: bfloat16 [2048, 1024], P(('pp', 'cp'), 'tp'), may hold values from -12 to 12
- values: bfloat16 [2048, 1024], P(('pp', 'cp'), 'tp'), may hold values from -6 to 6
- pair_order: int32 [4, 4], replicated, may hold values from 0 to 3, each once within a row
- lengths: int32 [4, 2], replicated, may hold values from 128 to 256
- routes: int32 [4, 512, 1], P(None, 'cp'), may hold values from 0 to 7; in each aligned block of 128 rows (0 to 127, 128 to 255, ..., all dimensions but the last counted through in order) at most 32 rows name the same one
Outputs:
- rebalanced: bfloat16 [4096, 16384], P(('pp', 'cp', 'tp'))
Inputs may be any that keep to these rules, and one draw needn't show every extreme that they name: `routes`: at most 32 rows of one device's block name the same destination, and in some block one destination is named by exactly 32 rows.
All inputs are finite; a program needn't handle non-finite values.
Results may differ from a plain program's by a relative error of at most 0.003.
Values may be sent and summed in bfloat16 or wider, within the bound.
No kernel may reach another device: no remote copies, remote signals or barrier semaphores. Data moves between devices by JAX's collectives and lax.ppermute only.
A program may use at most 64 MiB of HBM per device.

v0:
```python
import jax
import jax.numpy as jnp
from jax import lax
from jax.sharding import PartitionSpec as P

HD = 128
masked_score = -1e30


def shifted(block, axis, distance):
    devices = range(lax.axis_size(axis))
    route = [((i - distance) % len(devices), i) for i in devices]
    return lax.ppermute(block, axis, route)


def pair_positions(pair_ids, block_len, cycle_size):
    offsets = jnp.arange(block_len, dtype=jnp.int32)
    first_half = pair_ids[:, None] * block_len + offsets[None, :]
    second_half = (2 * cycle_size - 1 - pair_ids)[:, None] * block_len + offsets[None, :]
    return jnp.concatenate([first_half, second_half], axis=1)


def dispatch_rows(attended, targets, dest_count, capacity):
    row_count = attended.shape[0]
    matches = targets[:, None] == jnp.arange(dest_count, dtype=jnp.int32)[None, :]
    row_ids = jnp.arange(row_count, dtype=jnp.int32)
    earlier = (row_ids[None, :] < row_ids[:, None]).astype(jnp.bfloat16)
    before = jnp.dot(earlier, matches.astype(jnp.bfloat16), preferred_element_type=jnp.float32)
    slot_index = jnp.sum(jnp.where(matches, before, 0.0), axis=1).astype(jnp.int32)
    slot_ids = jnp.arange(capacity, dtype=jnp.int32)
    picked_rows = jnp.logical_and(
        jnp.transpose(matches)[:, None, :], slot_index[None, None, :] == slot_ids[None, :, None]
    )
    selector = picked_rows.astype(jnp.bfloat16).reshape(dest_count * capacity, row_count)
    return jnp.dot(selector, attended, preferred_element_type=jnp.float32).astype(jnp.bfloat16)


def spread_rows(buffer, cycle_size, split_size, capacity, width):
    flat_buffer = buffer.reshape(cycle_size * split_size, capacity, width)
    moved = lax.all_to_all(flat_buffer, ("cp", "tp"), split_axis=0, concat_axis=0, tiled=True)
    moved = jnp.transpose(moved.reshape(cycle_size, split_size, capacity, width), (0, 2, 1, 3))
    return moved.reshape(cycle_size * capacity, split_size * width)


def arrange_rows(attended, routes, source, cycle_size, split_size):
    row_count, width = attended.shape
    dest_count = cycle_size * split_size
    capacity = 2 * row_count // dest_count
    targets = lax.dynamic_index_in_dim(routes, source, 0, keepdims=False)[:, 0]
    buffer = dispatch_rows(attended, targets, dest_count, capacity)
    buffer = buffer.reshape(cycle_size, split_size, capacity, width)
    return spread_rows(buffer, cycle_size, split_size, capacity, width)


def body(queries, keys, values, pair_order, lengths, routes):
    cycle_size = lax.axis_size("cp")
    split_size = lax.axis_size("tp")
    section = lax.axis_index("pp")
    place = lax.axis_index("cp")
    row_count = queries.shape[0]
    block_len = row_count // 4
    width = queries.shape[1]
    group_count = keys.shape[1] // HD
    group_size = width // keys.shape[1]
    score_scale = HD ** (-0.5)
    order_row = lax.dynamic_index_in_dim(pair_order, section, 0, keepdims=False)
    own_pair = lax.dynamic_index_in_dim(order_row, place, 0, keepdims=True)
    query_pos = pair_positions(own_pair, block_len, cycle_size).reshape(2 * block_len)
    limits = lax.dynamic_index_in_dim(lengths, section, 0, keepdims=False)
    query_rows = queries.reshape(2, 2 * block_len, group_count, group_size, HD)
    stat_shape = (2, 2 * block_len, group_count, group_size)
    start_state = (
        jnp.full(stat_shape, masked_score, jnp.float32),
        jnp.zeros(stat_shape, jnp.float32),
        jnp.zeros(stat_shape + (HD,), jnp.float32),
    )
    state = start_state
    key_piece = lax.all_gather(keys, "cp", axis=0, tiled=True)
    value_piece = lax.all_gather(values, "cp", axis=0, tiled=True)
    shard_count = key_piece.shape[0] // row_count
    first_shard = jnp.int32(0) // row_count
    for base in range(0, shard_count, 4):
        block = min(4, shard_count - base)
        key_block = key_piece[base * row_count : (base + block) * row_count].reshape(
            block, 2, 2 * block_len, group_count, HD
        )
        value_block = value_piece[base * row_count : (base + block) * row_count].reshape(
            block, 2, 2 * block_len, group_count, HD
        )
        shard_ids = first_shard + base + jnp.arange(block, dtype=jnp.int32)
        key_pos = pair_positions(order_row[shard_ids], block_len, cycle_size).reshape(
            block * 2 * block_len
        )
        allowed = jnp.logical_and(
            key_pos[None, None, :] <= query_pos[None, :, None],
            key_pos[None, None, :] < limits[:, None, None],
        )
        allowed = allowed[:, :, None, None, :]
        scores = jnp.einsum(
            "sqgrd,nskgd->sqgrnk", query_rows, key_block, preferred_element_type=jnp.float32
        )
        scores = scores.reshape(stat_shape + (block * 2 * block_len,)) * score_scale
        running_max, running_total, running_sum = state
        block_max = jnp.max(jnp.where(allowed, scores, masked_score), axis=4)
        new_max = jnp.maximum(running_max, block_max)
        weights = jnp.where(allowed, jnp.exp(scores - new_max[..., None]), 0.0)
        carry_factor = jnp.exp(running_max - new_max)
        running_total = running_total * carry_factor + jnp.sum(weights, axis=4)
        shaped = weights.astype(jnp.bfloat16).reshape(stat_shape + (block, 2 * block_len))
        running_sum = running_sum * carry_factor[..., None] + jnp.einsum(
            "sqgrnk,nskgd->sqgrd", shaped, value_block, preferred_element_type=jnp.float32
        )
        state = (new_max, running_total, running_sum)
    attended = (state[2] / state[1][..., None]).astype(jnp.bfloat16).reshape(row_count, width)
    arranged = arrange_rows(attended, routes, section, cycle_size, split_size)
    return shifted(arranged, "pp", 1)


def solution(mesh):
    placed = (
        P(("pp", "cp"), "tp"),
        P(("pp", "cp"), "tp"),
        P(("pp", "cp"), "tp"),
        P(),
        P(),
        P(None, "cp", None),
    )
    return jax.shard_map(
        body, mesh=mesh, in_specs=placed, out_specs=P(("pp", "cp", "tp"), None), check_vma=False
    )
```

profile of v0, /device:TPU:0, one launch (start us, length us, event | category | flops | bytes accessed | tf_op | source)
XLA Modules:
  0.0 287.3 jit_solution(959507155664328261)
XLA Ops:
  0.0 0.7 copy-done
  0.7 0.1 fusion.9
  0.9 0.7 fusion.14
  1.6 1.3 dynamic_slice.18
  4.1 0.6 gather_fusion
  4.8 0.9 dynamic-slice_reduce_fusion
  5.7 0.1 add_bitcast_fusion
  5.7 0.1 iota_add_fusion
  5.8 0.1 pad_add_fusion
  5.9 0.1 broadcast_compare_fusion
  6.0 0.1 broadcast_compare_fusion.1
  6.1 2.2 copy.30
  8.3 17.4 %all_gather.6 = bf16[512,512]{1,0:T(8,128)(2,1)S(1)} all-gather(bf16[128,512]{1,0:T(8,128)(2,1)S(1)} %copy-done.2), channel_id=1, replica_groups=mesh['pp'=4,'cp'=4,'tp'=2] {'cp'}, dimensions={0}, use_global_device_ids=true | all-gather | bytes 655360 | tf_op jit(solution)/shard_map/all_gather | solution.py:78
  25.6 0.1 reshape.234
  25.8 0.1 broadcast_and_fusion
  25.9 5.5 %fusion = (f32[2,64,4,16]{1,3,2,0:T(8,128)S(1)}, f32[2,4,4,64,64,16]{4,3,5,2,1,0:T(8,128)S(1)}) fusion(pred[2,64,4,64]{1,3,2,0:T(8,128)(4,1)S(1)} %broadcast_and_fusion, bf16[2,64,4,16,128,1]{4,3,2,1,0,5:T(8,128)(2,1)S(1)} %bitcast.52, bf16[4,2,64,4,128,1]{4,3,2,1,0,5:T(4,128)(2,1)S(1)} %bitcast.54), kind=kOutput, calls=%fused_computation.3 | convolution fusion | flops 543154176 | bytes 11075584 | tf_op jit(solution)/shard_map/sqgrd,nskgd->sqgrnk/dot_general | solution.py:99
  31.4 6.2 %fusion.3 = (f32[2,64,4,16]{1,3,2,0:T(8,128)S(1)}, bf16[2,64,4,16,4,64]{1,5,3,4,2,0:T(8,128)(2,1)}) fusion(f32[2,4,4,64,64,16]{4,3,5,2,1,0:T(8,128)S(1)} %get-tuple-element.12, f32[2,64,4,16]{1,3,2,0:T(8,128)S(1)} %broadcast_maximum_fusion, pred[2,64,4,64]{1,3,2,0:T(8,128)(4,1)S(1)} %broadcast_and_fusion), kind=kLoop, calls=%fused_computation.6 | loop fusion | flops 10477568 | bytes 12681216 | tf_op jit(solution)/shard_map/reduce_sum | solution.py:108
  37.7 0.1 copy.14
  37.8 0.1 copy.17
  38.0 17.2 %copy.15 = bf16[2,64,4,16,4,64]{5,3,4,1,2,0:T(8,128)(2,1)} copy(bf16[2,64,4,16,4,64]{1,5,3,4,2,0:T(8,128)(2,1)} %get-tuple-element.6) | data formatting | bytes 8388608 | tf_op jit(solution)/shard_map/convert_element_type | solution.py:109
  55.2 16.2 %all_gather.7 = bf16[512,512]{1,0:T(8,128)(2,1)S(1)} all-gather(bf16[128,512]{1,0:T(8,128)(2,1)S(1)} %copy-done.3), channel_id=1, replica_groups=mesh['pp'=4,'cp'=4,'tp'=2] {'cp'}, dimensions={0}, use_global_device_ids=true | all-gather | bytes 655360 | tf_op jit(solution)/shard_map/all_gather | solution.py:79
  71.4 0.1 reshape.236
  71.6 5.7 %fusion.6 = bf16[2,64,4,16,128]{4,3,1,2,0:T(8,128)(2,1)S(1)} fusion(bf16[2,64,4,16,4,64]{5,3,4,1,2,0:T(8,128)(2,1)} %copy.15, f32[2,64,4,16]{3,1,2,0:T(8,128)S(1)} %copy.17, f32[2,64,4,16]{3,1,2,0:T(8,128)S(1)} %copy.14, bf16[4,2,64,4,128,1]{4,3,2,1,0,5:T(4,128)(2,1)S(1)} %bitcast.56), kind=kOutput, calls=%fused_computation.11 | convolution fusion | flops 540016640 | bytes 6881280 | tf_op jit(solution)/shard_map/sqgrnk,nskgd->sqgrd/dot_general | solution.py:110
  77.3 1.9 copy.18
  79.2 2.8 reshape.237
  82.1 1.2 convolution_convert_fusion
  83.3 97.9 %all_to_all.5 = bf16[8,32,8192]{2,1,0:T(8,128)(2,1)S(1)} all-to-all(bf16[8,32,8192]{2,1,0:T(8,128)(2,1)S(1)} %bitcast.49), channel_id=1, replica_groups=mesh['pp'=4,'cp'=4,'tp'=2] {'cp','tp'}, dimensions={0} | all-to-all | bytes 8388608 | tf_op jit(solution)/shard_map/all_to_all | solution.py:40
  181.2 6.4 %copy.19 = bf16[4,2,32,8192]{3,1,2,0:T(2,128)(2,1)} copy(bf16[4,2,32,8192]{3,2,1,0:T(8,128)(2,1)S(1)} %bitcast.50) | data formatting | bytes 8388608 | tf_op jit(solution)/shard_map/reshape | solution.py:41
  187.6 4.8 %copy.31 = bf16[16,8,2,8192]{3,1,2,0:T(8,128)(2,1)S(1)} copy(bf16[16,8,2,8192]{3,2,1,0:T(2,128)(2,1)} %bitcast.51) | data formatting | bytes 8388608
  192.4 1.6 collective-permute-start
  194.0 91.3 %collective-permute-done = bf16[128,16384]{1,0:T(8,128)(2,1)S(1)} collective-permute-done((bf16[128,16384]{1,0:T(8,128)(2,1)S(1)}, bf16[128,16384]{1,0:T(8,128)(2,1)S(1)}, u32[]{:S(2)}, u32[]{:S(2)}) %collective-permute-start) | collective-permute-done | bytes 4194336 | tf_op jit(solution)/shard_map/ppermute | solution.py:13
  285.3 2.0 copy.45
  (18 shorter events, 0.1 us)
Async XLA Ops:
  0.0 0.7 copy-start
  0.0 8.3 %copy-start.2 = (bf16[128,512]{1,0:T(8,128)(2,1)S(1)}, bf16[128,512]{1,0:T(8,128)(2,1)}, u32[]{:S(2)}) copy-start(bf16[128,512]{1,0:T(8,128)(2,1)} %param.7) | copy-start | bytes 393220
  38.0 17.2 %copy-start.3 = (bf16[128,512]{1,0:T(8,128)(2,1)S(1)}, bf16[128,512]{1,0:T(8,128)(2,1)}, u32[]{:S(2)}) copy-start(bf16[128,512]{1,0:T(8,128)(2,1)} %param.8) | copy-start | bytes 393220
  192.4 94.9 %copy-start.1 = (s32[4,128,1]{1,2,0:T(1,128)S(1)}, s32[4,128,1]{1,2,0:T(1,128)}, u32[]{:S(2)}) copy-start(s32[4,128,1]{1,2,0:T(1,128)} %param.11) | copy-start | bytes 6148
  192.4 92.9 %collective-permute-start = (bf16[128,16384]{1,0:T(8,128)(2,1)S(1)}, bf16[128,16384]{1,0:T(8,128)(2,1)S(1)}, u32[]{:S(2)}, u32[]{:S(2)}) collective-permute-start(bf16[128,16384]{1,0:T(8,128)(2,1)S(1)} %bitcast.53), channel_id=1, source_target_pairs={{24,0},{0,8},{8,16},{16,24},{25,1},{1,9},{9,17},{17,25},{26,2},{2,... | collective-permute-start | bytes 12582920 | tf_op jit(solution)/shard_map/ppermute | solution.py:13
where the time goes:
time: 288 us; the launch traced here: 287 us
  blocking collectives  131 us (45%)
  waiting for transfers between devices  91.3 us (32%)
  local copies, waits for them, and re-layouts  42 us (15%)
  matrix products  12.6 us (4%)
  other arithmetic  6.85 us (2%)
    all_to_all x1, blocking collectives, spread_rows(): lax.all_to_all(flat_buffer, ('cp', 'tp'), split_axis=0, concat_axis=0, ti...  97.9 us
    ppermute x1, waiting for transfers between devices, shifted(): return lax.ppermute(block, axis, route)  91.3 us
    all_gather x1, blocking collectives, body(): key_piece = lax.all_gather(keys, 'cp', axis=0, tiled=True)  17.4 us
    convert_element_type x1, local copies, waits for them, and re-layouts, body(): weights.astype(jnp.bfloat16).reshape(stat_shape + (block, 2 * block_len))  17.2 us
    all_gather x1, blocking collectives, body(): value_piece = lax.all_gather(values, 'cp', axis=0, tiled=True)  16.2 us
    unnamed x11, local copies, waits for them, and re-layouts  9.69 us
    reshape x1, local copies, waits for them, and re-layouts, spread_rows(): moved.reshape(cycle_size, split_size, capacity, width)  6.38 us
    reduce_sum x1, other arithmetic, body(): running_total = running_total * carry_factor + jnp.sum(weights, axis=4)  6.22 us
  transfers between devices with their start and end apart: 1, of which 1 were waited for; matrix products, arithmetic and copies ran while one was open for 0% of the time, Pallas kernels for 0%

commit v1 on v0

--- a/solution.py
+++ b/solution.py
@@ -75,7 +75,22 @@
         jnp.zeros(stat_shape + (HD,), jnp.float32),
     )
     state = start_state
-    key_piece = lax.all_gather(keys, "cp", axis=0, tiled=True)
+    ways, here, step = (lax.axis_size("cp"), lax.axis_index("cp"), keys.shape[0])
+    dims = [n * ways if d == 0 else n for d, n in enumerate(keys.shape)]
+    key_piece = lax.dynamic_update_slice_in_dim(
+        jnp.zeros(dims, keys.dtype), keys, here * step, axis=0
+    )
+    going_up = going_down = keys
+    for far in range(1, ways // 2 + 1):
+        going_up = lax.ppermute(going_up, "cp", [(d, (d + 1) % ways) for d in range(ways)])
+        key_piece = lax.dynamic_update_slice_in_dim(
+            key_piece, going_up, (here - far) % ways * step, axis=0
+        )
+        if 2 * far < ways:
+            going_down = lax.ppermute(going_down, "cp", [(d, (d - 1) % ways) for d in range(ways)])
+            key_piece = lax.dynamic_update_slice_in_dim(
+                key_piece, going_down, (here + far) % ways * step, axis=0
+            )
     value_piece = lax.all_gather(values, "cp", axis=0, tiled=True)
     shard_count = key_piece.shape[0] // row_count
     first_shard = jnp.int32(0) // row_count

time: 288 us -> 282 us (0.979)
  blocking collectives: 131 us -> 112 us
  waiting for transfers between devices: 91.3 us -> 97.7 us
  starting transfers between devices: 1.55 us -> 7.1 us
    all_gather x1 -> x0, blocking collectives: 17.4 us -> none  [body(): key_piece = lax.all_gather(keys, 'cp', axis=0, tiled=True)]
    ppermute x0 -> x3, waiting for transfers between devices: none -> 6.53 us  [the longest x2 6.53 us: body(): lax.ppermute(going_up, 'cp', [(d, (d + 1) % ways) for d in range(ways)])]
    ppermute x0 -> x3, starting transfers between devices: none -> 5.3 us  [the longest x2 3.22 us: body(): lax.ppermute(going_up, 'cp', [(d, (d + 1) % ways) for d in range(ways)])]
    unnamed x11 -> x9, local copies, waits for them, and re-layouts: 9.69 us -> 9.01 us
  transfers between devices with their start and end apart: 1 -> 4, of which waited for: 1 -> 2; matrix products, arithmetic and copies ran while one was open for 0% -> 3% of each run, Pallas kernels for 0% -> 0%
where the time goes in v1:
time: 282 us; the launch traced here: 281 us
  blocking collectives  112 us (40%)
  waiting for transfers between devices  97.7 us (35%)
  local copies, waits for them, and re-layouts  43.2 us (15%)
  matrix products  12.6 us (4%)
  starting transfers between devices  7.1 us (3%)
  other arithmetic  6.84 us (2%)
    all_to_all x1, blocking collectives, spread_rows(): lax.all_to_all(flat_buffer, ('cp', 'tp'), split_axis=0, concat_axis=0, ti...  96.5 us
    ppermute x1, waiting for transfers between devices, shifted(): return lax.ppermute(block, axis, route)  91.2 us
    convert_element_type x1, local copies, waits for them, and re-layouts, body(): weights.astype(jnp.bfloat16).reshape(stat_shape + (block, 2 * block_len))  17.2 us
    all_gather x1, blocking collectives, body(): value_piece = lax.all_gather(values, 'cp', axis=0, tiled=True)  15.8 us
    unnamed x9, local copies, waits for them, and re-layouts  9.01 us
    ppermute x2, waiting for transfers between devices, body(): lax.ppermute(going_up, 'cp', [(d, (d + 1) % ways) for d in range(ways)])  6.53 us
    reshape x1, local copies, waits for them, and re-layouts, spread_rows(): moved.reshape(cycle_size, split_size, capacity, width)  6.38 us
    reduce_sum x1, other arithmetic, body(): running_total = running_total * carry_factor + jnp.sum(weights, axis=4)  6.2 us
  transfers between devices with their start and end apart: 4, of which 2 were waited for; matrix products, arithmetic and copies ran while one was open for 3% of the time, Pallas kernels for 0%

profile of v1, /device:TPU:0, one launch (start us, length us, event | category | flops | bytes accessed | tf_op | source)
XLA Modules:
  0.0 281.2 jit_solution(9802608389377049211)
XLA Ops:
  0.0 3.0 %collective-permute-start = (bf16[128,512]{1,0:T(8,128)(2,1)}, bf16[128,512]{1,0:T(8,128)(2,1)S(1)}, u32[]{:S(2)}, u32[]{:S(2)}) collective-permute-start(bf16[128,512]{1,0:T(8,128)(2,1)} %param.7), channel_id=1, source_target_pairs={{0,2},{2,4},{4,6},{6,0},{1,3},{3,5},{5,7},{7,1},{8,10},{10,12},{12... | collective-permute-start | bytes 393224 | tf_op jit(solution)/shard_map/ppermute | solution.py:85
  3.0 2.1 collective-permute-start.1
  5.1 0.1 fusion.9
  5.3 0.7 fusion.15
  6.0 1.3 dynamic_slice.18
  8.6 0.6 gather_fusion
  9.2 0.9 fusion.13
  10.2 0.1 pad_add_fusion
  10.3 0.1 broadcast_compare_fusion
  10.5 0.1 broadcast_and_fusion
  10.7 15.8 %all_gather.3 = bf16[512,512]{1,0:T(8,128)(2,1)S(1)} all-gather(bf16[128,512]{1,0:T(8,128)(2,1)} %param.8), channel_id=1, replica_groups=mesh['pp'=4,'cp'=4,'tp'=2] {'cp'}, dimensions={0}, use_global_device_ids=true | all-gather | bytes 655360 | tf_op jit(solution)/shard_map/all_gather | solution.py:94
  26.5 0.9 constant_dynamic-update-slice_fusion.3
  27.5 2.2 copy.30
  29.7 0.9 reshape.236
  30.6 0.2 collective-permute-start.2
  30.8 6.5 %collective-permute-done.2 = bf16[128,512]{1,0:T(8,128)(2,1)S(1)} collective-permute-done((bf16[128,512]{1,0:T(8,128)(2,1)S(1)}, bf16[128,512]{1,0:T(8,128)(2,1)S(1)}, u32[]{:S(2)}, u32[]{:S(2)}) %collective-permute-start.2) | collective-permute-done | bytes 131104 | tf_op jit(solution)/shard_map/ppermute | solution.py:85
  37.4 0.1 reshape.234
  37.5 5.5 %fusion = (f32[2,64,4,16]{1,3,2,0:T(8,128)S(1)}, f32[2,4,4,64,64,16]{4,3,5,2,1,0:T(8,128)S(1)}) fusion(pred[2,64,4,64]{1,3,2,0:T(8,128)(4,1)S(1)} %broadcast_and_fusion, bf16[2,64,4,16,128,1]{4,3,2,1,0,5:T(8,128)(2,1)S(1)} %bitcast.52, bf16[4,2,64,4,128,1]{4,3,2,1,0,5:T(4,128)(2,1)S(1)} %bitcast.54), kind=kOutput, calls=%fused_computation.3 | convolution fusion | flops 543154176 | bytes 11075584 | tf_op jit(solution)/shard_map/sqgrd,nskgd->sqgrnk/dot_general | solution.py:114
  43.0 6.2 %fusion.3 = (f32[2,64,4,16]{1,3,2,0:T(8,128)S(1)}, bf16[2,64,4,16,4,64]{1,5,3,4,2,0:T(8,128)(2,1)}) fusion(f32[2,4,4,64,64,16]{4,3,5,2,1,0:T(8,128)S(1)} %get-tuple-element.12, f32[2,64,4,16]{1,3,2,0:T(8,128)S(1)} %broadcast_maximum_fusion, pred[2,64,4,64]{1,3,2,0:T(8,128)(4,1)S(1)} %broadcast_and_fusion), kind=kLoop, calls=%fused_computation.6 | loop fusion | flops 10477568 | bytes 12681216 | tf_op jit(solution)/shard_map/reduce_sum | solution.py:123
  49.3 0.1 copy.14
  49.4 0.1 copy.17
  49.5 17.2 %copy.15 = bf16[2,64,4,16,4,64]{5,3,4,1,2,0:T(8,128)(2,1)} copy(bf16[2,64,4,16,4,64]{1,5,3,4,2,0:T(8,128)(2,1)} %get-tuple-element.6) | data formatting | bytes 8388608 | tf_op jit(solution)/shard_map/convert_element_type | solution.py:124
  66.8 5.7 %fusion.6 = bf16[2,64,4,16,128]{4,3,1,2,0:T(8,128)(2,1)S(1)} fusion(bf16[2,64,4,16,4,64]{5,3,4,1,2,0:T(8,128)(2,1)} %copy.15, f32[2,64,4,16]{3,1,2,0:T(8,128)S(1)} %copy.17, f32[2,64,4,16]{3,1,2,0:T(8,128)S(1)} %copy.14, bf16[4,2,64,4,128,1]{4,3,2,1,0,5:T(4,128)(2,1)S(1)} %bitcast.56), kind=kOutput, calls=%fused_computation.11 | convolution fusion | flops 540016640 | bytes 6881280 | tf_op jit(solution)/shard_map/sqgrnk,nskgd->sqgrd/dot_general | solution.py:125
  72.5 1.9 copy.18
  74.4 2.8 %reshape.237 = bf16[128,8192]{1,0:T(8,128)(2,1)S(1)} reshape(bf16[2,64,4,16,128]{4,3,2,1,0:T(8,128)(2,1)} %copy.18) | data formatting | bytes 4194304 | tf_op jit(solution)/shard_map/reshape | solution.py:129
  77.3 1.2 convolution_convert_fusion
  78.5 96.5 %all_to_all.5 = bf16[8,32,8192]{2,1,0:T(8,128)(2,1)S(1)} all-to-all(bf16[8,32,8192]{2,1,0:T(8,128)(2,1)S(1)} %bitcast.49), channel_id=1, replica_groups=mesh['pp'=4,'cp'=4,'tp'=2] {'cp','tp'}, dimensions={0} | all-to-all | bytes 8388608 | tf_op jit(solution)/shard_map/all_to_all | solution.py:40
  175.0 6.4 %copy.19 = bf16[4,2,32,8192]{3,1,2,0:T(2,128)(2,1)} copy(bf16[4,2,32,8192]{3,2,1,0:T(8,128)(2,1)S(1)} %bitcast.50) | data formatting | bytes 8388608 | tf_op jit(solution)/shard_map/reshape | solution.py:41
  181.4 4.8 %copy.31 = bf16[16,8,2,8192]{3,1,2,0:T(8,128)(2,1)S(1)} copy(bf16[16,8,2,8192]{3,2,1,0:T(2,128)(2,1)} %bitcast.51) | data formatting | bytes 8388608
  186.2 1.8 collective-permute-start.3
  188.0 91.2 %collective-permute-done.3 = bf16[128,16384]{1,0:T(8,128)(2,1)S(1)} collective-permute-done((bf16[128,16384]{1,0:T(8,128)(2,1)S(1)}, bf16[128,16384]{1,0:T(8,128)(2,1)S(1)}, u32[]{:S(2)}, u32[]{:S(2)}) %collective-permute-start.3) | collective-permute-done | bytes 4194336 | tf_op jit(solution)/shard_map/ppermute | solution.py:13
  279.2 2.0 copy.49
  (26 shorter events, 0.4 us)
Async XLA Ops:
  0.0 5.1 %copy-start = (s32[4,128,1]{1,2,0:T(1,128)S(1)}, s32[4,128,1]{1,2,0:T(1,128)}, u32[]{:S(2)}) copy-start(s32[4,128,1]{1,2,0:T(1,128)} %param.11) | copy-start | bytes 6148
  0.0 30.6 %collective-permute-start = (bf16[128,512]{1,0:T(8,128)(2,1)}, bf16[128,512]{1,0:T(8,128)(2,1)S(1)}, u32[]{:S(2)}, u32[]{:S(2)}) collective-permute-start(bf16[128,512]{1,0:T(8,128)(2,1)} %param.7), channel_id=1, source_target_pairs={{0,2},{2,4},{4,6},{6,0},{1,3},{3,5},{5,7},{7,1},{8,10},{10,12},{12... | collective-permute-start | bytes 393224 | tf_op jit(solution)/shard_map/ppermute | solution.py:85
  3.0 27.8 %collective-permute-start.1 = (bf16[128,512]{1,0:T(8,128)(2,1)}, bf16[128,512]{1,0:T(8,128)(2,1)S(1)}, u32[]{:S(2)}, u32[]{:S(2)}) collective-permute-start(bf16[128,512]{1,0:T(8,128)(2,1)} %param.7), channel_id=1, source_target_pairs={{0,6},{2,0},{4,2},{6,4},{1,7},{3,1},{5,3},{7,5},{8,14},{10,8},{12,... | collective-permute-start | bytes 393224 | tf_op jit(solution)/shard_map/ppermute | solution.py:90
  30.6 6.8 %collective-permute-start.2 = (bf16[128,512]{1,0:T(8,128)(2,1)S(1)}, bf16[128,512]{1,0:T(8,128)(2,1)S(1)}, u32[]{:S(2)}, u32[]{:S(2)}) collective-permute-start(bf16[128,512]{1,0:T(8,128)(2,1)S(1)} %collective-permute-done), channel_id=1, source_target_pairs={{0,2},{2,4},{4,6},{6,0},{1,3},{3,5},{5,7},{7,1},{8,10},{10,12},{12... | collective-permute-start | bytes 393224 | tf_op jit(solution)/shard_map/ppermute | solution.py:85
  49.5 17.2 %copy-start.2 = (bf16[4,2,64,4,128]{4,3,2,1,0:T(4,128)(2,1)S(1)}, bf16[4,2,64,4,128]{4,3,2,1,0:T(4,128)(2,1)}, u32[]{:S(2)}) copy-start(bf16[4,2,64,4,128]{4,3,2,1,0:T(4,128)(2,1)} %reshape.236) | copy-start | bytes 1572868
  186.2 95.0 %copy-start.1 = (s32[4,128,1]{1,2,0:T(1,128)S(1)}, s32[4,128,1]{1,2,0:T(1,128)}, u32[]{:S(2)}) copy-start(s32[4,128,1]{1,2,0:T(1,128)} %param.11) | copy-start | bytes 6148
  186.2 93.0 %collective-permute-start.3 = (bf16[128,16384]{1,0:T(8,128)(2,1)S(1)}, bf16[128,16384]{1,0:T(8,128)(2,1)S(1)}, u32[]{:S(2)}, u32[]{:S(2)}) collective-permute-start(bf16[128,16384]{1,0:T(8,128)(2,1)S(1)} %bitcast.53), channel_id=1, source_target_pairs={{24,0},{0,8},{8,16},{16,24},{25,1},{1,9},{9,17},{17,25},{26,2},{2,... | collective-permute-start | bytes 12582920 | tf_op jit(solution)/shard_map/ppermute | solution.py:13
